TPU v7x, 1024 devices: a whole 4x8x16 slice. The times are simulated.
1024 devices in a mesh: energy: 128 (over x, z_hi, y, core), slab: 8 (over z_lo).
Axes of the slice: x: 4, y: 8, z: 16 (z_hi: 2, z_lo: 8; z = z_hi * 8 + z_lo), core: 2. Of those that a mesh axis runs over, the one named last changes fastest.
Arguments:
- green: bfloat16 [128, 8, 2, 384, 384], P('energy', 'slab'), may hold values from -6 to 6
- weights: int32 [128, 2, 2], P('energy'), may hold values from 1 to 63
- coupling_m: bfloat16 [2, 384, 384], replicated, may hold values from -0.3125 to 0.3125
- coupling_n: bfloat16 [2, 384, 384], replicated, may hold values from -0.3125 to 0.3125
Outputs:
- sigma: bfloat16 [128, 8, 2, 384, 384], P('energy', 'slab')
All inputs are finite; a program needn't handle non-finite values.
Results may differ from a plain program's by a relative error of at most 0.0061.
Values may be sent and summed in bfloat16 or wider, within the bound.
A program may use at most 32 MiB of HBM per device.

v0:
```python
import jax
import jax.numpy as jnp
from jax import lax
from jax.sharding import PartitionSpec as P

K1 = 3
K2 = 7


def from_behind(block, axis, distance):
    devices = range(lax.axis_size(axis))
    route = [(i - distance, i) for i in devices if i - distance in devices]
    return lax.ppermute(block, axis, route)


def combine(upper, lower, wrow):
    mixed = wrow[0] * upper.astype(jnp.float32) + wrow[1] * lower.astype(jnp.float32)
    return mixed.astype(jnp.bfloat16)


def coupled(mat, combo):
    left = jnp.einsum("ij,pjk->pik", mat, combo, preferred_element_type=jnp.float32).astype(
        jnp.bfloat16
    )
    return jnp.einsum("pik,lk->pil", left, mat, preferred_element_type=jnp.float32)


def body(green, weights, coupling_m, coupling_n):
    scaled = weights[0].astype(jnp.float32) / 32.0
    near_upper = from_behind(green, "energy", -K1)
    near_lower = from_behind(green, "energy", K1)
    far_upper = from_behind(green, "energy", -K2)
    far_lower = from_behind(green, "energy", K2)
    combos = (
        combine(near_upper[0, 0], near_lower[0, 0], scaled[0]),
        combine(far_upper[0, 0], far_lower[0, 0], scaled[1]),
    )
    own = coupled(coupling_m[0], combos[0]) + coupled(coupling_m[1], combos[1])
    term = coupled(coupling_n[0], combos[0]) + coupled(coupling_n[1], combos[1])
    term = term.astype(jnp.bfloat16)[None, None]
    arrived = from_behind(term, "slab", -1)
    total = own[None, None] + arrived.astype(jnp.float32)
    return total.astype(jnp.bfloat16)


def solution(mesh):
    placed = (P("energy", "slab", None, None, None), P("energy", None, None), P(), P())
    return jax.shard_map(
        body,
        mesh=mesh,
        in_specs=placed,
        out_specs=P("energy", "slab", None, None, None),
        check_vma=False,
    )
```

profile of v0, /device:TPU:346, one launch (start us, length us, event | category | flops | bytes accessed | tf_op | source)
XLA Modules:
  0.0 210.6 jit_solution(510376493512587958)
XLA Ops:
  0.0 1.9 collective-permute-start
  1.9 4.9 %collective-permute-start.1 = (bf16[1,1,2,384,384]{4,3,2,1,0:T(8,128)(2,1)}, bf16[1,1,2,384,384]{4,3,2,1,0:T(8,128)(2,1)S(1)}, u32[]{:S(2)}, u32[]{:S(2)}) collective-permute-start(bf16[1,1,2,384,384]{4,3,2,1,0:T(8,128)(2,1)} %param.4), channel_id=1, source_target_pairs={{0,24},{8,32},{16,40},{24,48},{32,56},{40,64},{48,72},{56,80},{64,... | collective-permute-start | bytes 1769480 | tf_op jit(solution)/shard_map/ppermute | solution.py:13
  6.8 27.0 %collective-permute-start.2 = (bf16[1,1,2,384,384]{4,3,2,1,0:T(8,128)(2,1)}, bf16[1,1,2,384,384]{4,3,2,1,0:T(8,128)(2,1)S(1)}, u32[]{:S(2)}, u32[]{:S(2)}) collective-permute-start(bf16[1,1,2,384,384]{4,3,2,1,0:T(8,128)(2,1)} %param.4), channel_id=1, source_target_pairs={{56,0},{64,8},{72,16},{80,24},{88,32},{96,40},{104,48},{112,56},{1... | collective-permute-start | bytes 1769480 | tf_op jit(solution)/shard_map/ppermute | solution.py:13
  33.8 1.9 collective-permute-start.3
  35.8 0.7 multiply_bitcast_fusion
  36.4 0.7 fusion.35
  37.1 0.0 collective-permute-done
  37.1 0.0 collective-permute-done.1
  37.1 0.0 copy-start
  37.1 4.3 %fusion.7 = f32[2,384,384]{2,1,0:T(8,128)} fusion(bf16[2,384,384]{2,1,0:T(8,128)(2,1)} %param.7, bf16[1,1,2,384,384]{4,3,2,1,0:T(8,128)(2,1)S(1)} %collective-permute-done.1, bf16[1,1,2,384,384]{4,3,2,1,0:T(8,128)(2,1)S(1)} %collective-permute-done, f32[]{:T(128)} %bitcast.2, f32[]{:T(128)} %bitcast.1), kind=kOutput, calls=%fused_computation.13 | convolution fusion | flops 455049216 | bytes 2949128 | tf_op jit(solution)/shard_map/pik,lk->pil/dot_general | solution.py:25
  41.4 11.0 %collective-permute-done.2 = bf16[1,1,2,384,384]{4,3,2,1,0:T(8,128)(2,1)S(1)} collective-permute-done((bf16[1,1,2,384,384]{4,3,2,1,0:T(8,128)(2,1)}, bf16[1,1,2,384,384]{4,3,2,1,0:T(8,128)(2,1)S(1)}, u32[]{:S(2)}, u32[]{:S(2)}) %collective-permute-start.2) | collective-permute-done | bytes 589856 | tf_op jit(solution)/shard_map/ppermute | solution.py:13
  52.3 88.4 %collective-permute-done.3 = bf16[1,1,2,384,384]{4,3,2,1,0:T(8,128)(2,1)S(1)} collective-permute-done((bf16[1,1,2,384,384]{4,3,2,1,0:T(8,128)(2,1)}, bf16[1,1,2,384,384]{4,3,2,1,0:T(8,128)(2,1)S(1)}, u32[]{:S(2)}, u32[]{:S(2)}) %collective-permute-start.3) | collective-permute-done | bytes 589856 | tf_op jit(solution)/shard_map/ppermute | solution.py:13
  140.8 0.0 copy-done
  140.8 0.0 copy-start.1
  140.8 4.3 %fusion.2 = bf16[1,1,2,384,384]{4,3,2,1,0:T(8,128)(2,1)} fusion(f32[2,384,384]{2,1,0:T(8,128)} %fusion.7, bf16[2,384,384]{2,1,0:T(8,128)(2,1)S(1)} %copy-done, bf16[1,1,2,384,384]{4,3,2,1,0:T(8,128)(2,1)S(1)} %collective-permute-done.3, bf16[1,1,2,384,384]{4,3,2,1,0:T(8,128)(2,1)S(1)} %collective-permute-done.2, f32[]{:T(128)} %bitcast.8, f32[]{:T(128)} %bitcast.7), kind=kOutput, calls=%fused_computation.8 | convolution fusion | flops 455639040 | bytes 3538952 | tf_op jit(solution)/shard_map/pik,lk->pil/dot_general | solution.py:25
  145.0 19.4 %collective-permute-start.4 = (bf16[1,1,2,384,384]{4,3,2,1,0:T(8,128)(2,1)}, bf16[1,1,2,384,384]{4,3,2,1,0:T(8,128)(2,1)S(1)}, u32[]{:S(2)}, u32[]{:S(2)}) collective-permute-start(bf16[1,1,2,384,384]{4,3,2,1,0:T(8,128)(2,1)} %fusion.2), channel_id=1, source_target_pairs={{1,0},{2,1},{3,2},{4,3},{5,4},{6,5},{7,6},{9,8},{10,9},{11,10},{12... | collective-permute-start | bytes 1769480 | tf_op jit(solution)/shard_map/ppermute | solution.py:13
  164.5 0.0 copy-done.1
  164.5 3.1 %fusion.4 = f32[2,384,384]{2,1,0:T(8,128)} fusion(bf16[2,384,384]{2,1,0:T(8,128)(2,1)S(1)} %copy-done.1, bf16[1,1,2,384,384]{4,3,2,1,0:T(8,128)(2,1)S(1)} %collective-permute-done.1, bf16[1,1,2,384,384]{4,3,2,1,0:T(8,128)(2,1)S(1)} %collective-permute-done, f32[]{:T(128)} %bitcast.2, f32[]{:T(128)} %bitcast.1), kind=kOutput, calls=%fused_computation.10 | convolution fusion | flops 455049216 | bytes 2949128 | tf_op jit(solution)/shard_map/pik,lk->pil/dot_general | solution.py:25
  167.7 38.8 %collective-permute-done.4 = bf16[1,1,2,384,384]{4,3,2,1,0:T(8,128)(2,1)S(1)} collective-permute-done((bf16[1,1,2,384,384]{4,3,2,1,0:T(8,128)(2,1)}, bf16[1,1,2,384,384]{4,3,2,1,0:T(8,128)(2,1)S(1)}, u32[]{:S(2)}, u32[]{:S(2)}) %collective-permute-start.4) | collective-permute-done | bytes 589856 | tf_op jit(solution)/shard_map/ppermute | solution.py:13
  206.4 4.2 %add_convert_fusion = bf16[1,1,2,384,384]{4,3,2,1,0:T(8,128)(2,1)} fusion(bf16[1,1,2,384,384]{4,3,2,1,0:T(8,128)(2,1)S(1)} %collective-permute-done.4, f32[2,384,384]{2,1,0:T(8,128)} %fusion.4, bf16[2,384,384]{2,1,0:T(8,128)(2,1)S(1)} %copy-done.1, bf16[1,1,2,384,384]{4,3,2,1,0:T(8,128)(2,1)S(1)} %collective-permute-done.3, ...), kind=kOutput, calls=%fused_computation.15 | convolution fusion | flops 456228864 | bytes 4128776 | tf_op jit(solution)/shard_map/pik,lk->pil/dot_general | solution.py:25
Async XLA Ops:
  0.0 37.1 %collective-permute-start = (bf16[1,1,2,384,384]{4,3,2,1,0:T(8,128)(2,1)}, bf16[1,1,2,384,384]{4,3,2,1,0:T(8,128)(2,1)S(1)}, u32[]{:S(2)}, u32[]{:S(2)}) collective-permute-start(bf16[1,1,2,384,384]{4,3,2,1,0:T(8,128)(2,1)} %param.4), channel_id=1, source_target_pairs={{24,0},{32,8},{40,16},{48,24},{56,32},{64,40},{72,48},{80,56},{88,... | collective-permute-start | bytes 1769480 | tf_op jit(solution)/shard_map/ppermute | solution.py:13
  1.9 35.2 %collective-permute-start.1 = (bf16[1,1,2,384,384]{4,3,2,1,0:T(8,128)(2,1)}, bf16[1,1,2,384,384]{4,3,2,1,0:T(8,128)(2,1)S(1)}, u32[]{:S(2)}, u32[]{:S(2)}) collective-permute-start(bf16[1,1,2,384,384]{4,3,2,1,0:T(8,128)(2,1)} %param.4), channel_id=1, source_target_pairs={{0,24},{8,32},{16,40},{24,48},{32,56},{40,64},{48,72},{56,80},{64,... | collective-permute-start | bytes 1769480 | tf_op jit(solution)/shard_map/ppermute | solution.py:13
  6.8 45.6 %collective-permute-start.2 = (bf16[1,1,2,384,384]{4,3,2,1,0:T(8,128)(2,1)}, bf16[1,1,2,384,384]{4,3,2,1,0:T(8,128)(2,1)S(1)}, u32[]{:S(2)}, u32[]{:S(2)}) collective-permute-start(bf16[1,1,2,384,384]{4,3,2,1,0:T(8,128)(2,1)} %param.4), channel_id=1, source_target_pairs={{56,0},{64,8},{72,16},{80,24},{88,32},{96,40},{104,48},{112,56},{1... | collective-permute-start | bytes 1769480 | tf_op jit(solution)/shard_map/ppermute | solution.py:13
  33.8 106.9 %collective-permute-start.3 = (bf16[1,1,2,384,384]{4,3,2,1,0:T(8,128)(2,1)}, bf16[1,1,2,384,384]{4,3,2,1,0:T(8,128)(2,1)S(1)}, u32[]{:S(2)}, u32[]{:S(2)}) collective-permute-start(bf16[1,1,2,384,384]{4,3,2,1,0:T(8,128)(2,1)} %param.4), channel_id=1, source_target_pairs={{0,56},{8,64},{16,72},{24,80},{32,88},{40,96},{48,104},{56,112},{6... | collective-permute-start | bytes 1769480 | tf_op jit(solution)/shard_map/ppermute | solution.py:13
  37.1 103.7 %copy-start = (bf16[2,384,384]{2,1,0:T(8,128)(2,1)S(1)}, bf16[2,384,384]{2,1,0:T(8,128)(2,1)}, u32[]{:S(2)}) copy-start(bf16[2,384,384]{2,1,0:T(8,128)(2,1)} %param.7) | copy-start | bytes 1769476
  140.8 23.7 %copy-start.1 = (bf16[2,384,384]{2,1,0:T(8,128)(2,1)S(1)}, bf16[2,384,384]{2,1,0:T(8,128)(2,1)}, u32[]{:S(2)}) copy-start(bf16[2,384,384]{2,1,0:T(8,128)(2,1)} %param.6) | copy-start | bytes 1769476
  145.0 61.4 %collective-permute-start.4 = (bf16[1,1,2,384,384]{4,3,2,1,0:T(8,128)(2,1)}, bf16[1,1,2,384,384]{4,3,2,1,0:T(8,128)(2,1)S(1)}, u32[]{:S(2)}, u32[]{:S(2)}) collective-permute-start(bf16[1,1,2,384,384]{4,3,2,1,0:T(8,128)(2,1)} %fusion.2), channel_id=1, source_target_pairs={{1,0},{2,1},{3,2},{4,3},{5,4},{6,5},{7,6},{9,8},{10,9},{11,10},{12... | collective-permute-start | bytes 1769480 | tf_op jit(solution)/shard_map/ppermute | solution.py:13
where the time goes:
time: 211 us
  waiting for transfers between devices  138 us (65%)
  starting transfers between devices  55.2 us (26%)
  matrix products  15.9 us (8%)
    ppermute x5, waiting for transfers between devices, from_behind(): return lax.ppermute(block, axis, route)  138 us
    ppermute x5, starting transfers between devices, from_behind(): return lax.ppermute(block, axis, route)  55.2 us
    dot_general x4, matrix products, coupled(): jnp.einsum('pik,lk->pil', left, mat, preferred_element_type=jnp.float32)  15.9 us
  transfers between devices with their start and end apart: 5, of which 3 were waited for; matrix products, arithmetic and copies ran while one was open for 4% of the time, Pallas kernels for 0%

commit v1 on v0

v1 whole, which is shorter than its diff:
```python
import functools

import jax
import jax.numpy as jnp
from jax import lax
from jax.experimental import pallas as pl
from jax.experimental.pallas import tpu as pltpu
from jax.sharding import PartitionSpec as P

MESH = pl.DeviceIdType.MESH
RUN = 16
ROWS = 128
A, B, C, D, IMG = range(5)
F32, BF16 = jnp.float32, jnp.bfloat16


def kernel(
    energies,
    slabs,
    green,
    weights,
    coup_m,
    coup_n,
    out,
    held,
    own,
    term,
    term_out,
    term_in,
    right,
    left_m,
    left_n,
    send_sem,
    recv_sem,
    term_send,
    term_recv,
):
    e, s = lax.axis_index("energy"), lax.axis_index("slab")
    size = green.shape[-1]
    per_part = size // ROWS
    chunks = 2 * per_part
    run, p = lax.div(e, RUN), lax.rem(e, RUN)
    first, last = run == 0, run == energies // RUN - 1

    def at(shift):
        return (run * RUN + lax.rem(p + shift + RUN, RUN), s)

    def both(*conds):
        return functools.reduce(jnp.logical_and, conds)

    def either(a, b):
        return jnp.logical_or(a, b)

    inner_up, inner_down = p >= 9, p <= 6
    has_up = both(inner_up, jnp.logical_not(first))
    has_down = both(inner_down, jnp.logical_not(last))
    has_image = either(has_up, has_down)
    got = {A: e >= 3, B: e >= 7, C: e < energies - 3, D: e < energies - 7}

    up_own, down_own = p + 3 < RUN, p >= 3
    sends = {
        "near_up": (either(up_own, has_up), at(3), A),
        "near_down": (either(down_own, has_down), at(-3), C),
        "relay_up": (both(p + 4 < RUN, got[A]), at(4), B),
        "relay_down": (both(p >= 4, got[C]), at(-4), D),
        "far_up": (both(has_up, p <= 12), at(7), B),
        "far_down": (both(has_down, p >= 3), at(-7), D),
        "image_up": (both(inner_up, jnp.logical_not(last)), (e + RUN, s), IMG),
        "image_down": (both(inner_down, jnp.logical_not(first)), (e - RUN, s), IMG),
    }
    number = {name: i for i, name in enumerate(sends)}
    term_goes, term_comes = s > 0, s < slabs - 1

    sources = [
        (got[A], at(-3)),
        (got[C], at(3)),
        (both(got[B], p >= 4), at(-4)),
        (both(got[B], p < 4), at(-7)),
        (both(got[D], p + 4 < RUN), at(4)),
        (both(got[D], p + 4 >= RUN), at(7)),
        (has_up, (e - RUN, s)),
        (has_down, (e + RUN, s)),
        (term_comes, (e, s + 1)),
    ]
    barrier = pltpu.get_barrier_semaphore()
    for cond, where in sources:

        @pl.when(cond)
        def _():
            pl.semaphore_signal(barrier, inc=1, device_id=where, device_id_type=MESH)

    count = sum(cond.astype(jnp.int32) for cond, _, _ in sends.values())
    pl.semaphore_wait(barrier, count + term_goes.astype(jnp.int32))

    def piece(ref, c):
        return ref.at[lax.div(c, per_part), pl.ds(lax.rem(c, per_part) * ROWS, ROWS)]

    def copy(name, source, c):
        _, where, slot = sends[name]
        i = number[name]
        return pltpu.make_async_remote_copy(
            piece(source, c),
            piece(held.at[slot], c),
            send_sem.at[i, c],
            recv_sem.at[slot, c],
            device_id=where,
            device_id_type=MESH,
        )

    def arrived(slot, c):
        pltpu.make_async_remote_copy(
            piece(held.at[slot], c),
            piece(held.at[slot], c),
            send_sem.at[0, c],
            recv_sem.at[slot, c],
            device_id=at(3),
            device_id_type=MESH,
        ).wait_recv()

    mine = green.at[0, 0]

    def start(name, cond, source, c):
        @pl.when(cond)
        def _():
            copy(name, source, c).start()

    @pl.loop(0, chunks)
    def _(c):
        start("image_up", sends["image_up"][0], mine, c)
        start("image_down", sends["image_down"][0], mine, c)
        start("near_up", up_own, mine, c)
        start("near_down", down_own, mine, c)

    for slot, there in got.items():

        @pl.when(jnp.logical_not(there))
        def _():
            held[slot] = jnp.zeros(held.shape[1:], BF16)

    @pl.when(jnp.logical_not(term_comes))
    def _():
        term_in[...] = jnp.zeros_like(term_in)

    for m in range(2):
        right[m, :, :size] = coup_m[m].T
        right[m, :, size:] = coup_n[m].T
        for r in range(per_part):
            rows = slice(r * ROWS, (r + 1) * ROWS)
            cols = slice(m * ROWS, (m + 1) * ROWS)
            left_m[r, :, cols] = coup_m[m, :, rows]
            left_n[r, :, cols] = coup_n[m, :, rows]

    def forward(c):
        @pl.when(has_image)
        def _():
            arrived(IMG, c)

        image = held.at[IMG]
        start("near_up", both(jnp.logical_not(up_own), has_up), image, c)
        start("near_down", both(jnp.logical_not(down_own), has_down), image, c)
        start("far_up", sends["far_up"][0], image, c)
        start("far_down", sends["far_down"][0], image, c)

        @pl.when(got[A])
        def _():
            arrived(A, c)

        start("relay_up", sends["relay_up"][0], held.at[A], c)

        @pl.when(got[C])
        def _():
            arrived(C, c)

        start("relay_down", sends["relay_down"][0], held.at[C], c)

    def scale(m, i):
        return weights[0, m, i].astype(F32) / 32.0

    def term_copy(part):
        return pltpu.make_async_remote_copy(
            term_out.at[part],
            term_in.at[part],
            term_send.at[part],
            term_recv.at[part],
            device_id=(e, s - 1),
            device_id_type=MESH,
        )

    def compute(c):
        for slot in (B, D):

            @pl.when(got[slot])
            def _():
                arrived(slot, c)

        part, r = lax.div(c, per_part), lax.rem(c, per_part)
        rows = pl.ds(r * ROWS, ROWS)

        def half(m, upper, lower):
            mixed = scale(m, 0) * held[upper, part, rows].astype(F32)
            mixed += scale(m, 1) * held[lower, part, rows].astype(F32)
            return jnp.dot(
                mixed.astype(BF16), right[m], preferred_element_type=F32
            ).astype(BF16)

        both_modes = jnp.concatenate([half(0, C, A), half(1, D, B)], axis=0)
        add_term = jnp.dot(left_n[r], both_modes[:, size:], preferred_element_type=F32)

        @pl.when(r == 0)
        def _():
            term[...] = add_term

        @pl.when(r > 0)
        def _():
            term[...] += add_term

        @pl.when(r == per_part - 1)
        def _():
            term_out[part] = term[...].astype(BF16)

            @pl.when(term_goes)
            def _():
                term_copy(part).start()

        add_own = jnp.dot(left_m[r], both_modes[:, :size], preferred_element_type=F32)

        @pl.when(r == 0)
        def _():
            own[part] = add_own

        @pl.when(r > 0)
        def _():
            own[part] += add_own

    @pl.loop(0, chunks + 1)
    def _(c):
        @pl.when(c < chunks)
        def _():
            forward(c)

        @pl.when(c > 0)
        def _():
            compute(c - 1)

    for part in range(2):

        @pl.when(term_comes)
        def _():
            term_copy(part).wait_recv()

        out[0, 0, part] = (own[part] + term_in[part].astype(F32)).astype(BF16)

        @pl.when(term_goes)
        def _():
            term_copy(part).wait_send()

    @pl.loop(0, chunks)
    def _(c):
        for name, (cond, _, _) in sends.items():

            @pl.when(cond)
            def _():
                copy(name, mine, c).wait_send()


def solution(mesh):
    energies, slabs = mesh.shape["energy"], mesh.shape["slab"]

    def body(green, weights, coupling_m, coupling_n):
        size = green.shape[-1]
        per_part = size // ROWS
        vmem = pl.BlockSpec(memory_space=pltpu.VMEM)
        block = (2, size, size)
        return pl.pallas_call(
            functools.partial(kernel, energies, slabs),
            out_shape=jax.ShapeDtypeStruct(green.shape, BF16),
            in_specs=[vmem, pl.BlockSpec(memory_space=pltpu.SMEM), vmem, vmem],
            out_specs=vmem,
            scratch_shapes=[
                pltpu.VMEM((5, *block), BF16),
                pltpu.VMEM(block, F32),
                pltpu.VMEM((size, size), F32),
                pltpu.VMEM(block, BF16),
                pltpu.VMEM(block, BF16),
                pltpu.VMEM((2, size, 2 * size), BF16),
                pltpu.VMEM((per_part, size, 2 * ROWS), BF16),
                pltpu.VMEM((per_part, size, 2 * ROWS), BF16),
                pltpu.SemaphoreType.DMA((8, 2 * per_part)),
                pltpu.SemaphoreType.DMA((5, 2 * per_part)),
                pltpu.SemaphoreType.DMA((2,)),
                pltpu.SemaphoreType.DMA((2,)),
            ],
            compiler_params=pltpu.CompilerParams(collective_id=0, has_side_effects=True),
        )(green, weights, coupling_m, coupling_n)

    placed = (P("energy", "slab", None, None, None), P("energy", None, None), P(), P())
    return jax.shard_map(
        body,
        mesh=mesh,
        in_specs=placed,
        out_specs=P("energy", "slab", None, None, None),
        check_vma=False,
    )
```

time: 211 us -> 119 us (0.56)
  waiting for transfers between devices: 138 us -> 0 us
  Pallas kernels: 0 us -> 117 us
  starting transfers between devices: 55.2 us -> 0 us
  matrix products: 15.9 us -> 0 us
    ppermute x5 -> x0, waiting for transfers between devices: 138 us -> none  [from_behind(): return lax.ppermute(block, axis, route)]
    pallas_call x0 -> x1, Pallas kernels: none -> 117 us  [body(): pl.pallas_call(functools.partial(kernel, energies, slabs), out_shape=jax....]
    ppermute x5 -> x0, starting transfers between devices: 55.2 us -> none  [from_behind(): return lax.ppermute(block, axis, route)]
    dot_general x4 -> x0, matrix products: 15.9 us -> none  [coupled(): jnp.einsum('pik,lk->pil', left, mat, preferred_element_type=jnp.float32)]
  transfers between devices with their start and end apart: 5 -> 0, of which waited for: 3 -> 0; matrix products, arithmetic and copies ran while one was open for 4% -> 0% of each run, Pallas kernels for 0% -> 0%
where the time goes in v1:
time: 119 us
  Pallas kernels  117 us (98%)
  local copies, waits for them, and re-layouts  1.94 us (2%)
    pallas_call x1, Pallas kernels, body(): pl.pallas_call(functools.partial(kernel, energies, slabs), out_shape=jax....  117 us

profile of v1, /device:TPU:346, one launch (start us, length us, event | category | flops | bytes accessed | tf_op | source)
XLA Modules:
  0.0 118.6 jit_solution(13345346178600607849)
XLA Ops:
  0.0 116.7 %shard_map.46 = bf16[1,1,2,384,384]{4,3,2,1,0:T(8,128)(2,1)} custom-call(bf16[1,1,2,384,384]{4,3,2,1,0:T(8,128)(2,1)} %green.1, s32[1,2,2]{2,1,0:T(2,128)} %weights.1, bf16[2,384,384]{2,1,0:T(8,128)(2,1)} %coup_m.1, bf16[2,384,384]{2,1,0:T(8,128)(2,1)} %coup_n.1), custom_call_target="tpu_custom_call" | custom-call | tf_op jit(solution)/shard_map/pallas_call | solution.py:274
  116.7 1.9 %copy.6 = bf16[1,1,2,384,384]{4,3,2,1,0:T(8,128)(2,1)} copy(bf16[1,1,2,384,384]{4,3,2,1,0:T(8,128)(2,1)} %shard_map.46) | data formatting | bytes 1179648

commit v2 on v1

--- a/solution.py
+++ b/solution.py
@@ -10,6 +10,10 @@
 MESH = pl.DeviceIdType.MESH
 RUN = 16
 ROWS = 128
+LEAD = 2
+AHEAD = 2
+LATER = 2
+HALF = ROWS // 2
 A, B, C, D, IMG = range(5)
 F32, BF16 = jnp.float32, jnp.bfloat16
 
@@ -23,6 +27,7 @@
     coup_n,
     out,
     held,
+    passing,
     own,
     term,
     term_out,
@@ -32,6 +37,8 @@
     left_n,
     send_sem,
     recv_sem,
+    z_send,
+    z_recv,
     term_send,
     term_recv,
 ):
@@ -65,11 +72,37 @@
         "relay_down": (both(p >= 4, got[C]), at(-4), D),
         "far_up": (both(has_up, p <= 12), at(7), B),
         "far_down": (both(has_down, p >= 3), at(-7), D),
-        "image_up": (both(inner_up, jnp.logical_not(last)), (e + RUN, s), IMG),
-        "image_down": (both(inner_down, jnp.logical_not(first)), (e - RUN, s), IMG),
     }
     number = {name: i for i, name in enumerate(sends)}
     term_goes, term_comes = s > 0, s < slabs - 1
+
+    ring = 2 * slabs
+    quarter = ring // 4
+    runs = energies // RUN
+    x, z = lax.div(run, 2), lax.rem(run, 2) * slabs + s
+    step = jnp.where(inner_up, 1, -1)
+
+    def run_of(x_there, z_there):
+        return 2 * x_there + lax.div(z_there, slabs)
+
+    def device(x_there, z_there):
+        return (run_of(x_there, z_there) * RUN + p, lax.rem(z_there, slabs))
+
+    def around(shift):
+        return lax.rem(z + shift + ring, ring)
+
+    def gives(r):
+        up = both(inner_up, r < runs - 1)
+        return either(up, both(inner_down, r > 0))
+
+    ways = (quarter, -quarter)
+    gives_image = gives(run)
+    behind = [run_of(x, around(-w)) for w in ways]
+    passes = [gives(r) for r in behind]
+    pass_to = [
+        device(lax.div(r + step, 2), around(w)) for r, w in zip(behind, ways)
+    ]
+    x_source = lax.div(run - step + 2, 2) - 1
 
     sources = [
         (got[A], at(-3)),
@@ -78,8 +111,10 @@
         (both(got[B], p < 4), at(-7)),
         (both(got[D], p + 4 < RUN), at(4)),
         (both(got[D], p + 4 >= RUN), at(7)),
-        (has_up, (e - RUN, s)),
-        (has_down, (e + RUN, s)),
+        (passes[0], device(x, around(-ways[0]))),
+        (passes[1], device(x, around(-ways[1]))),
+        (has_image, device(x_source, around(-ways[0]))),
+        (has_image, device(x_source, around(-ways[1]))),
         (term_comes, (e, s + 1)),
     ]
     barrier = pltpu.get_barrier_semaphore()
@@ -89,8 +124,9 @@
         def _():
             pl.semaphore_signal(barrier, inc=1, device_id=where, device_id_type=MESH)
 
-    count = sum(cond.astype(jnp.int32) for cond, _, _ in sends.values())
-    pl.semaphore_wait(barrier, count + term_goes.astype(jnp.int32))
+    going = [cond for cond, _, _ in sends.values()]
+    going += [term_goes, gives_image, gives_image, *passes]
+    pl.semaphore_wait(barrier, sum(cond.astype(jnp.int32) for cond in going))
 
     def piece(ref, c):
         return ref.at[lax.div(c, per_part), pl.ds(lax.rem(c, per_part) * ROWS, ROWS)]
@@ -119,15 +155,39 @@
 
     mine = green.at[0, 0]
 
+    def half_of(ref, c, h):
+        first_row = lax.rem(c, per_part) * ROWS + h * HALF
+        return ref.at[lax.div(c, per_part), pl.ds(first_row, HALF)]
+
+    def z_copy(leg, h, c):
+        source = half_of(mine, c, h) if leg == 0 else passing.at[h, c]
+        target = passing.at[h, c] if leg == 0 else half_of(held.at[IMG], c, h)
+        return pltpu.make_async_remote_copy(
+            source,
+            target,
+            z_send.at[leg, h, c],
+            z_recv.at[leg, h, c],
+            device_id=device(x, around(ways[h])) if leg == 0 else pass_to[h],
+            device_id_type=MESH,
+        )
+
     def start(name, cond, source, c):
         @pl.when(cond)
         def _():
             copy(name, source, c).start()
 
+    def give(c):
+        @pl.when(gives_image)
+        def _():
+            for h in range(2):
+                z_copy(0, h, c).start()
+
     @pl.loop(0, chunks)
     def _(c):
-        start("image_up", sends["image_up"][0], mine, c)
-        start("image_down", sends["image_down"][0], mine, c)
+        @pl.when(c < AHEAD)
+        def _():
+            give(c)
+
         start("near_up", up_own, mine, c)
         start("near_down", down_own, mine, c)
 
@@ -153,7 +213,8 @@
     def forward(c):
         @pl.when(has_image)
         def _():
-            arrived(IMG, c)
+            for h in range(2):
+                z_copy(1, h, c).wait_recv()
 
         image = held.at[IMG]
         start("near_up", both(jnp.logical_not(up_own), has_up), image, c)
@@ -161,17 +222,13 @@
         start("far_up", sends["far_up"][0], image, c)
         start("far_down", sends["far_down"][0], image, c)
 
-        @pl.when(got[A])
-        def _():
-            arrived(A, c)
-
-        start("relay_up", sends["relay_up"][0], held.at[A], c)
-
-        @pl.when(got[C])
-        def _():
-            arrived(C, c)
-
-        start("relay_down", sends["relay_down"][0], held.at[C], c)
+    def relay(c, from_up, from_down):
+        for name, slot, cond in (("relay_up", A, from_up), ("relay_down", C, from_down)):
+
+            @pl.when(both(sends[name][0], cond))
+            def _():
+                arrived(slot, c)
+                copy(name, held.at[slot], c).start()
 
     def scale(m, i):
         return weights[0, m, i].astype(F32) / 32.0
@@ -187,9 +244,10 @@
         )
 
     def compute(c):
-        for slot in (B, D):
-
-            @pl.when(got[slot])
+        relayed = {A: sends["relay_up"][0], C: sends["relay_down"][0]}
+        for slot, there in got.items():
+
+            @pl.when(both(there, jnp.logical_not(relayed.get(slot, False))))
             def _():
                 arrived(slot, c)
 
@@ -232,15 +290,35 @@
         def _():
             own[part] += add_own
 
-    @pl.loop(0, chunks + 1)
+    lag = LEAD + LATER
+
+    @pl.loop(0, chunks + lag + 1)
     def _(c):
         @pl.when(c < chunks)
         def _():
-            forward(c)
-
-        @pl.when(c > 0)
-        def _():
-            compute(c - 1)
+            relay(c, down_own, up_own)
+            for h in range(2):
+
+                @pl.when(passes[h])
+                def _():
+                    z_copy(0, h, c).wait_recv()
+                    z_copy(1, h, c).start()
+
+            @pl.when(c + AHEAD < chunks)
+            def _():
+                give(c + AHEAD)
+
+        @pl.when(both(c >= LEAD, c < chunks + LEAD))
+        def _():
+            forward(c - LEAD)
+
+        @pl.when(both(c >= lag, c < chunks + lag))
+        def _():
+            relay(c - lag, jnp.logical_not(down_own), jnp.logical_not(up_own))
+
+        @pl.when(c > lag)
+        def _():
+            compute(c - lag - 1)
 
     for part in range(2):
 
@@ -261,6 +339,16 @@
             @pl.when(cond)
             def _():
                 copy(name, mine, c).wait_send()
+
+        for h in range(2):
+
+            @pl.when(gives_image)
+            def _():
+                z_copy(0, h, c).wait_send()
+
+            @pl.when(passes[h])
+            def _():
+                z_copy(1, h, c).wait_send()
 
 
 def solution(mesh):
@@ -278,6 +366,7 @@
             out_specs=vmem,
             scratch_shapes=[
                 pltpu.VMEM((5, *block), BF16),
+                pltpu.VMEM((2, 2 * per_part, HALF, size), BF16),
                 pltpu.VMEM(block, F32),
                 pltpu.VMEM((size, size), F32),
                 pltpu.VMEM(block, BF16),
@@ -285,8 +374,10 @@
                 pltpu.VMEM((2, size, 2 * size), BF16),
                 pltpu.VMEM((per_part, size, 2 * ROWS), BF16),
                 pltpu.VMEM((per_part, size, 2 * ROWS), BF16),
-                pltpu.SemaphoreType.DMA((8, 2 * per_part)),
-                pltpu.SemaphoreType.DMA((5, 2 * per_part)),
+                pltpu.SemaphoreType.DMA((6, 2 * per_part)),
+                pltpu.SemaphoreType.DMA((4, 2 * per_part)),
+                pltpu.SemaphoreType.DMA((2, 2, 2 * per_part)),
+                pltpu.SemaphoreType.DMA((2, 2, 2 * per_part)),
                 pltpu.SemaphoreType.DMA((2,)),
                 pltpu.SemaphoreType.DMA((2,)),
             ],

time: 119 us -> 115 us (0.966)
  the two profiles are of different devices: /device:TPU:346 before, /device:TPU:156 now
where the time goes in v2:
time: 115 us
  Pallas kernels  113 us (98%)
  local copies, waits for them, and re-layouts  1.94 us (2%)
    pallas_call x1, Pallas kernels, body(): pl.pallas_call(functools.partial(kernel, energies, slabs), out_shape=jax....  113 us

profile of v2, /device:TPU:156, one launch (start us, length us, event | category | flops | bytes accessed | tf_op | source)
XLA Modules:
  0.0 115.2 jit_solution(1901420179299090791)
XLA Ops:
  0.0 113.2 %shard_map.46 = bf16[1,1,2,384,384]{4,3,2,1,0:T(8,128)(2,1)} custom-call(bf16[1,1,2,384,384]{4,3,2,1,0:T(8,128)(2,1)} %green.1, s32[1,2,2]{2,1,0:T(2,128)} %weights.1, bf16[2,384,384]{2,1,0:T(8,128)(2,1)} %coup_m.1, bf16[2,384,384]{2,1,0:T(8,128)(2,1)} %coup_n.1), custom_call_target="tpu_custom_call" | custom-call | tf_op jit(solution)/shard_map/pallas_call | solution.py:362
  113.2 1.9 %copy.6 = bf16[1,1,2,384,384]{4,3,2,1,0:T(8,128)(2,1)} copy(bf16[1,1,2,384,384]{4,3,2,1,0:T(8,128)(2,1)} %shard_map.46) | data formatting | bytes 1179648

commit v3 on v2

--- a/solution.py
+++ b/solution.py
@@ -296,7 +296,6 @@
     def _(c):
         @pl.when(c < chunks)
         def _():
-            relay(c, down_own, up_own)
             for h in range(2):
 
                 @pl.when(passes[h])
@@ -311,6 +310,10 @@
         @pl.when(both(c >= LEAD, c < chunks + LEAD))
         def _():
             forward(c - LEAD)
+
+        @pl.when(c < chunks)
+        def _():
+            relay(c, down_own, up_own)
 
         @pl.when(both(c >= lag, c < chunks + lag))
         def _():

time: 115 us -> 116 us (level)
  no operation moved by 1% of the time
where the time goes in v3:
time: 116 us
  Pallas kernels  114 us (98%)
  local copies, waits for them, and re-layouts  1.94 us (2%)
    pallas_call x1, Pallas kernels, body(): pl.pallas_call(functools.partial(kernel, energies, slabs), out_shape=jax....  114 us

profile of v3, /device:TPU:156, one launch (start us, length us, event | category | flops | bytes accessed | tf_op | source)
XLA Modules:
  0.0 115.6 jit_solution(10633435574902077701)
XLA Ops:
  0.0 113.7 %shard_map.46 = bf16[1,1,2,384,384]{4,3,2,1,0:T(8,128)(2,1)} custom-call(bf16[1,1,2,384,384]{4,3,2,1,0:T(8,128)(2,1)} %green.1, s32[1,2,2]{2,1,0:T(2,128)} %weights.1, bf16[2,384,384]{2,1,0:T(8,128)(2,1)} %coup_m.1, bf16[2,384,384]{2,1,0:T(8,128)(2,1)} %coup_n.1), custom_call_target="tpu_custom_call" | custom-call | tf_op jit(solution)/shard_map/pallas_call | solution.py:365
  113.7 1.9 %copy.6 = bf16[1,1,2,384,384]{4,3,2,1,0:T(8,128)(2,1)} copy(bf16[1,1,2,384,384]{4,3,2,1,0:T(8,128)(2,1)} %shard_map.46) | data formatting | bytes 1179648
